TPU v7x, 128 devices: a whole 4x4x4 slice. The times are simulated.
128 devices in a mesh: row: 8 (over x, y_hi), col: 16 (over y_lo, z, core).
Axes of the slice: x: 4, y: 4 (y_hi: 2, y_lo: 2; y = y_hi * 2 + y_lo), z: 4, core: 2. Of those that a mesh axis runs over, the one named last changes fastest.
Arguments:
- front_trailing: float32 [16384, 16384], P('row', 'col'), may hold values from -6 to 6
- panel_columns: float32 [16384, 1024], P('row', 'col'), may hold values from -0.1875 to 0.1875
- panel_rows: float32 [1024, 16384], P('row', 'col'), may hold values from -6 to 6
- pivots: int32 [1024], replicated, may hold values from 0 to 1023, each once
- diag_inverse: float32 [1024, 1024], replicated, may hold values from -0.1875 to 0.1875
- test_matrix: float32 [16384, 512], P('col'), may hold values from -0.046875 to 0.046875
Outputs:
- schur: float32 [16384, 16384], P('row', 'col')
- off_samples: float32 [16384, 512], P(('row', 'col'))
- leaf_blocks: float32 [16384, 128], P(('row', 'col'))
- group_gram: float32 [8, 512, 512], P('row')
Inputs may be any that keep to these rules, and one draw needn't show every extreme that they name: pivots names each of 0 to 1023 once.
All inputs are finite; a program needn't handle non-finite values.
Results may differ from a plain program's by a relative error of at most 0.000084.
Values sent between devices are 32-bit elements; how exact they have to be, the bound alone decides.
A program may use at most 128 MiB of HBM per device.

v0:
```python
import jax
import jax.numpy as jnp
from jax import lax
from jax.sharding import PartitionSpec as P

LEAF = 128


def product(left, right):
    return jnp.dot(left, right, precision=lax.Precision.HIGH, preferred_element_type=jnp.float32)


def body(front_trailing, panel_columns, panel_rows, pivots, diag_inverse, test_matrix):
    col_count = lax.axis_size("col")
    row_count = lax.axis_size("row")
    row_index = lax.axis_index("row")
    col_index = lax.axis_index("col")
    height, width = front_trailing.shape
    upper_full = lax.all_gather(panel_rows, "row", axis=0, tiled=True)
    left = lax.all_gather(panel_columns, "col", axis=1, tiled=True)
    upper = jnp.take(upper_full, pivots, axis=0)
    weight = product(diag_inverse, upper)
    schur = front_trailing - product(left, weight)
    rows = row_index * height + jnp.arange(height, dtype=jnp.int32)
    cols = col_index * width + jnp.arange(width, dtype=jnp.int32)
    same_leaf = rows[:, None] // LEAF == cols[None, :] // LEAF
    masked = jnp.where(same_leaf, jnp.zeros_like(schur), schur)
    partial = product(masked, test_matrix)
    count = width // LEAF
    ratio = col_count // row_count
    leaves = height // LEAF
    kept = []
    for leaf in range(leaves):
        held = col_index == row_index * ratio + leaf // count
        block = schur[
            leaf * LEAF : (leaf + 1) * LEAF, leaf % count * LEAF : (leaf % count + 1) * LEAF
        ]
        kept.append(jnp.where(held, block, jnp.zeros_like(block)))
    both = jnp.concatenate([partial, jnp.concatenate(kept, axis=0)], axis=1)
    own = lax.psum_scatter(both, "col", scatter_dimension=0, tiled=True)
    own_samples = own[:, : partial.shape[1]]
    leaf_blocks = own[:, partial.shape[1] :]
    gram = lax.dot_general(
        own_samples,
        own_samples,
        (((0,), (0,)), ((), ())),
        precision=lax.Precision.HIGH,
        preferred_element_type=jnp.float32,
    )
    gram = lax.psum(gram, "col")
    route = [(i, i ^ 1) for i in range(row_count)]
    gram = gram + lax.ppermute(gram, "row", route)
    group_gram = (gram / (2 * height))[None]
    return (schur, own_samples, leaf_blocks, group_gram)


def solution(mesh):
    placed = (P("row", "col"), P("row", "col"), P("row", "col"), P(), P(), P("col", None))
    return jax.shard_map(
        body,
        mesh=mesh,
        in_specs=placed,
        out_specs=(
            P("row", "col"),
            P(("row", "col"), None),
            P(("row", "col"), None),
            P("row", None, None),
        ),
        check_vma=False,
    )
```

profile of v0, /device:TPU:0, one launch (start us, length us, event | category | flops | bytes accessed | tf_op | source)
XLA Modules:
  0.0 392.7 jit_solution(6487991175751841340)
XLA Ops:
  7.2 0.0 all-gather.3.cloned.1.call-start
  7.2 0.7 all-gather.3.cloned.1.call-update
  7.9 0.0 all-gather.5.cloned.1.call-start
  8.0 0.7 all-gather.5.cloned.1.call-update
  8.7 0.0 reduce-scatter.2.cloned.1.call-start
  8.7 9.1 %copy.10 = f32[2048,1024]{0,1:T(8,128)} copy(f32[2048,1024]{1,0:T(8,128)} %param.6) | data formatting | bytes 16777216 | tf_op args[0]
  17.9 66.5 %all-gather.3.cloned.1.call-done = f32[1024,1024]{1,0:T(8,128)} async-done(((f32[128,1024]{1,0:T(8,128)}), f32[1024,1024]{1,0:T(8,128)}) %all-gather.3.cloned.1.call-update) | async-done | bytes 4194320 | tf_op jit(solution)/shard_map/all_gather | solution.py:19
  84.4 8.6 %gather_fusion = f32[1024,1024]{1,0:T(8,128)} fusion(f32[1024,1024]{1,0:T(8,128)} %all-gather.3.cloned.1.call-done, s32[1024]{0:T(1024)S(1)} %fusion.32), kind=kCustom, calls=%fused_computation | custom fusion | bytes 8392704 | tf_op jit(solution)/shard_map/jit(_take)/gather | solution.py:21
  93.0 17.9 %fusion.5 = f32[1024,1024]{1,0:T(8,128)} fusion(f32[1024,1024]{1,0:T(8,128)} %param.10, f32[1024,1024]{1,0:T(8,128)} %gather_fusion, pred[1024]{0:T(1024)(128)(4,1)S(1)} %compare_and_fusion), kind=kOutput, calls=%fused_computation.8 | convolution fusion | flops 6443499520 | bytes 12583936 | tf_op jit(solution)/shard_map/dot_general | solution.py:10
  110.9 25.2 %all-gather.5.cloned.1.call-done = f32[2048,1024]{0,1:T(8,128)} async-done(((f32[2048,64]{0,1:T(8,128)}), f32[2048,1024]{0,1:T(8,128)}) %all-gather.5.cloned.1.call-update) | async-done | bytes 8388624 | tf_op jit(solution)/shard_map/all_gather | solution.py:20
  136.1 17.8 %bitcast_subtract_fusion = f32[2048,1024]{0,1:T(8,128)S(1)} fusion(f32[2048,1024]{0,1:T(8,128)} %copy.10, f32[1024,1024]{1,0:T(8,128)} %fusion.5, f32[2048,1024]{0,1:T(8,128)} %all-gather.5.cloned.1.call-done), kind=kOutput, calls=%fused_computation.1 | convolution fusion | flops 12886999040 | bytes 29360128 | tf_op jit(solution)/shard_map/dot_general | solution.py:10
  154.3 7.6 %fusion = f32[2048,512]{0,1:T(8,128)S(1)} fusion(f32[1024,512]{1,0:T(8,128)S(1)} %copy-done, f32[2048,1024]{0,1:T(8,128)S(1)} %bitcast_subtract_fusion, s32[2048]{0:T(1024)S(1)} %add_select_fusion, s32[1024]{0:T(1024)S(1)} %add_select_fusion.1), kind=kOutput, calls=%fused_computation.2 | convolution fusion | flops 6446645248 | bytes 14692352 | tf_op jit(solution)/shard_map/dot_general | solution.py:10
  161.9 3.0 pad_maximum_fusion
  164.9 0.0 reduce-scatter.2.cloned.1.call-update
  164.9 0.0 all-reduce.2.cloned.1.call-start
  165.0 70.5 %reduce-scatter.2.cloned.1.call-done = f32[128,640]{0,1:T(8,128)} async-done(((f32[2048,640]{0,1:T(8,128)}), f32[128,640]{0,1:T(8,128)}) %reduce-scatter.2.cloned.1.call-update) | async-done | bytes 327696 | tf_op jit(solution)/shard_map/reduce_scatter | solution.py:40
  235.5 2.6 fusion.35
  238.1 119.0 %all-reduce.2.cloned.1.call-done = f32[512,512]{1,0:T(8,128)} async-done(((f32[512,512]{1,0:T(8,128)}), f32[512,512]{1,0:T(8,128)}) %all-reduce.2.cloned.1.call-update) | async-done | bytes 1048592 | tf_op jit(solution)/shard_map/psum | solution.py:50
  357.1 2.7 collective-permute-start
  359.8 9.2 %copy.11 = f32[2048,1024]{1,0:T(8,128)} copy(f32[2048,1024]{0,1:T(8,128)} %copy-done.1) | data formatting | bytes 16777216
  369.1 0.8 copy.12
  369.9 0.7 copy.13
  370.6 13.1 %collective-permute-done = f32[512,512]{1,0:T(8,128)} collective-permute-done((f32[512,512]{1,0:T(8,128)}, f32[512,512]{1,0:T(8,128)}, u32[]{:S(2)}, u32[]{:S(2)}) %collective-permute-start) | collective-permute-done | bytes 1048608 | tf_op jit(solution)/shard_map/ppermute | solution.py:52
  383.7 2.4 multiply_bitcast_fusion
  (33 shorter events, 0.3 us)
Async XLA Ops:
  7.2 147.1 %copy-start = (f32[1024,512]{1,0:T(8,128)S(1)}, f32[1024,512]{1,0:T(8,128)}, u32[]{:S(2)}) copy-start(f32[1024,512]{1,0:T(8,128)} %param.11) | copy-start | bytes 6291460
  7.2 77.2 %all-gather.3.cloned.1.call-start = ((), (), s32[]{:S(2)}) async-start(), calls=%async_computation.1 | async-start | bytes 4718592 | tf_op jit(solution)/shard_map/all_gather | solution.py:19
  7.9 128.2 %all-gather.5.cloned.1.call-start = ((), (), s32[]{:S(2)}) async-start(), calls=%async_computation.2 | async-start | bytes 8912896 | tf_op jit(solution)/shard_map/all_gather | solution.py:20
  8.7 226.8 %reduce-scatter.2.cloned.1.call-start = ((), (), s32[]{:S(2)}) async-start(), calls=%async_computation.3 | async-start | bytes 5570560 | tf_op jit(solution)/shard_map/reduce_scatter | solution.py:40
  8.7 9.2 %copy-start.3 = (s32[1024]{0:T(1024)S(1)}, s32[1024]{0:T(1024)}, u32[]{:S(2)}) copy-start(s32[1024]{0:T(1024)} %param.9) | copy-start | bytes 12292
  154.0 7.9 %copy-start.1 = (f32[2048,1024]{0,1:T(8,128)}, f32[2048,1024]{0,1:T(8,128)S(1)}, u32[]{:S(2)}) copy-start(f32[2048,1024]{0,1:T(8,128)S(1)} %bitcast_subtract_fusion) | copy-start | bytes 25165828
  164.9 192.2 %all-reduce.2.cloned.1.call-start = ((), (), s32[]{:S(2)}) async-start(), calls=%async_computation.4 | async-start | bytes 2097152 | tf_op jit(solution)/shard_map/psum | solution.py:50
  238.1 131.0 %slice-start = ((f32[128,640]{0,1:T(8,128)}), f32[128,512]{0,1:T(8,128)S(1)}, s32[]{:S(2)}) async-start(f32[128,640]{0,1:T(8,128)} %reduce-scatter.2.cloned.1.call-done), calls=%async_computation.5 | async-start | bytes 524288 | tf_op jit(solution)/shard_map/slice | solution.py:41
  238.1 131.8 %slice-start.1 = ((f32[128,640]{0,1:T(8,128)}), f32[128,128]{0,1:T(8,128)S(1)}, s32[]{:S(2)}) async-start(f32[128,640]{0,1:T(8,128)} %reduce-scatter.2.cloned.1.call-done), calls=%async_computation.6 | async-start | bytes 131072 | tf_op jit(solution)/shard_map/slice | solution.py:42
  357.1 26.6 %copy-start.2 = (f32[512,512]{1,0:T(8,128)S(1)}, f32[512,512]{1,0:T(8,128)}, u32[]{:S(2)}) copy-start(f32[512,512]{1,0:T(8,128)} %all-reduce.2.cloned.1.call-done) | copy-start | bytes 3145732
  357.1 26.6 %collective-permute-start = (f32[512,512]{1,0:T(8,128)}, f32[512,512]{1,0:T(8,128)}, u32[]{:S(2)}, u32[]{:S(2)}) collective-permute-start(f32[512,512]{1,0:T(8,128)} %all-reduce.2.cloned.1.call-done), channel_id=1, source_target_pairs={{0,16},{16,0},{32,48},{48,32},{64,80},{80,64},{96,112},{112,96},{1... | collective-permute-start | bytes 3145736 | tf_op jit(solution)/shard_map/ppermute | solution.py:52
Sparse Core Ops, SparseCore 0:
  10.3 74.0 all-gather.2
  86.1 49.9 all-gather.4
  165.0 70.3 reduce-scatter.1
  238.4 118.7 all-reduce.1
where the time goes:
time: 393 us
  waiting for transfers between devices  296 us (75%)
  matrix products  45.9 us (12%)
  local copies, waits for them, and re-layouts  28.6 us (7%)
  between operations  14 us (4%)
  other arithmetic  5.64 us (1%)
    psum x1, waiting for transfers between devices, body(): gram = lax.psum(gram, 'col')  119 us
    reduce_scatter x1, waiting for transfers between devices, body(): own = lax.psum_scatter(both, 'col', scatter_dimension=0, tiled=True)  70.5 us
    all_gather x1, waiting for transfers between devices, body(): upper_full = lax.all_gather(panel_rows, 'row', axis=0, tiled=True)  66.5 us
    dot_general x3, matrix products, product(): jnp.dot(left, right, precision=lax.Precision.HIGH, preferred_element_type...  43.3 us
    all_gather x1, waiting for transfers between devices, body(): left = lax.all_gather(panel_columns, 'col', axis=1, tiled=True)  25.2 us
    unnamed x12, local copies, waits for them, and re-layouts  20 us
    ppermute x1, waiting for transfers between devices, body(): gram = gram + lax.ppermute(gram, 'row', route)  13.1 us
    gather x1, local copies, waits for them, and re-layouts, body(): upper = jnp.take(upper_full, pivots, axis=0)  8.63 us
  transfers between devices with their start and end apart: 5, of which 5 were waited for; matrix products, arithmetic and copies ran while one was open for 12% of the time, Pallas kernels for 0%

commit v1 on v0

--- a/solution.py
+++ b/solution.py
@@ -17,7 +17,7 @@
     col_index = lax.axis_index("col")
     height, width = front_trailing.shape
     upper_full = lax.all_gather(panel_rows, "row", axis=0, tiled=True)
-    left = lax.all_gather(panel_columns, "col", axis=1, tiled=True)
+    left = jnp.concatenate(lax.all_gather(panel_columns, axis_name="col"), axis=1)
     upper = jnp.take(upper_full, pivots, axis=0)
     weight = product(diag_inverse, upper)
     schur = front_trailing - product(left, weight)

time: 393 us -> 410 us (1.043)
  local copies, waits for them, and re-layouts: 28.6 us -> 45 us
    unnamed x12 -> x17, local copies, waits for them, and re-layouts: 20 us -> 28.2 us
    reshape x0 -> x1, local copies, waits for them, and re-layouts: none -> 8.09 us  [body(): jnp.concatenate(lax.all_gather(panel_columns, axis_name='col'), axis=1)]
  transfers between devices with their start and end apart: 5 -> 5, of which waited for: 5 -> 5; matrix products, arithmetic and copies ran while one was open for 12% -> 11% of each run, Pallas kernels for 0% -> 0%
where the time goes in v1:
time: 410 us; the launch traced here: 409 us
  waiting for transfers between devices  296 us (72%)
  matrix products  45.9 us (11%)
  local copies, waits for them, and re-layouts  45 us (11%)
  between operations  14 us (3%)
  other arithmetic  5.64 us (1%)
    psum x1, waiting for transfers between devices, body(): gram = lax.psum(gram, 'col')  119 us
    reduce_scatter x1, waiting for transfers between devices, body(): own = lax.psum_scatter(both, 'col', scatter_dimension=0, tiled=True)  70.6 us
    all_gather x1, waiting for transfers between devices, body(): upper_full = lax.all_gather(panel_rows, 'row', axis=0, tiled=True)  66.5 us
    dot_general x3, matrix products, product(): jnp.dot(left, right, precision=lax.Precision.HIGH, preferred_element_type...  43.3 us
    unnamed x17, local copies, waits for them, and re-layouts  28.2 us
    all_gather x1, waiting for transfers between devices, body(): lax.all_gather(panel_columns, axis_name='col')  25.2 us
    ppermute x1, waiting for transfers between devices, body(): gram = gram + lax.ppermute(gram, 'row', route)  13.1 us
    gather x1, local copies, waits for them, and re-layouts, body(): upper = jnp.take(upper_full, pivots, axis=0)  8.63 us
  transfers between devices with their start and end apart: 5, of which 5 were waited for; matrix products, arithmetic and copies ran while one was open for 11% of the time, Pallas kernels for 0%

profile of v1, /device:TPU:0, one launch (start us, length us, event | category | flops | bytes accessed | tf_op | source)
XLA Modules:
  0.0 409.4 jit_solution(7802697801661590909)
XLA Ops:
  7.2 0.7 all-gather.4.cloned.1.call-update
  7.9 0.0 all-gather.6.cloned.1.call-start
  8.0 0.7 all-gather.6.cloned.1.call-update
  8.7 0.0 reduce-scatter.2.cloned.1.call-start
  8.7 9.1 %copy.19 = f32[2048,1024]{0,1:T(8,128)} copy(f32[2048,1024]{1,0:T(8,128)} %param.6) | data formatting | bytes 16777216 | tf_op args[0]
  17.9 66.5 %all-gather.4.cloned.1.call-done = f32[1024,1024]{1,0:T(8,128)} async-done(((f32[128,1024]{1,0:T(8,128)}), f32[1024,1024]{1,0:T(8,128)}) %all-gather.4.cloned.1.call-update) | async-done | bytes 4194320 | tf_op jit(solution)/shard_map/all_gather | solution.py:19
  84.4 8.6 %gather_fusion = f32[1024,1024]{1,0:T(8,128)} fusion(f32[1024,1024]{1,0:T(8,128)} %all-gather.4.cloned.1.call-done, s32[1024]{0:T(1024)S(1)} %fusion.32), kind=kCustom, calls=%fused_computation | custom fusion | bytes 8392704 | tf_op jit(solution)/shard_map/jit(_take)/gather | solution.py:21
  93.0 17.9 %fusion.5 = f32[1024,1024]{1,0:T(8,128)} fusion(f32[1024,1024]{1,0:T(8,128)} %param.10, f32[1024,1024]{1,0:T(8,128)} %gather_fusion, pred[1024]{0:T(1024)(128)(4,1)S(1)} %compare_and_fusion), kind=kOutput, calls=%fused_computation.8 | convolution fusion | flops 6443499520 | bytes 12583936 | tf_op jit(solution)/shard_map/dot_general | solution.py:10
  110.9 25.2 %all-gather.6.cloned.1.call-done = f32[32768,64]{0,1:T(8,128)} async-done(((f32[2048,64]{0,1:T(8,128)}), f32[32768,64]{0,1:T(8,128)}) %all-gather.6.cloned.1.call-update) | async-done | bytes 8388624 | tf_op jit(solution)/shard_map/all_gather | solution.py:20
  136.1 8.3 %copy.23 = f32[8,8,16,2048]{3,2,1,0:T(8,128)S(1)} copy(f32[8,8,16,2048]{3,1,2,0:T(8,128)} %bitcast.16) | data formatting | bytes 16777216
  144.4 8.1 %copy.18 = f32[2048,16,64]{0,2,1:T(8,128)} copy(f32[2048,16,64]{0,1,2:T(8,128)S(1)} %bitcast.15) | data formatting | bytes 16777216 | tf_op jit(solution)/shard_map/reshape | solution.py:20
  152.5 17.9 %bitcast_subtract_fusion = f32[2048,1024]{0,1:T(8,128)S(1)} fusion(f32[2048,1024]{0,1:T(8,128)S(1)} %bitcast.18, f32[1024,1024]{1,0:T(8,128)} %fusion.5, f32[2048,1024]{0,1:T(8,128)} %bitcast.19), kind=kOutput, calls=%fused_computation.1 | convolution fusion | flops 12886999040 | bytes 29360128 | tf_op jit(solution)/shard_map/dot_general | solution.py:10
  170.7 7.6 %fusion = f32[2048,512]{0,1:T(8,128)S(1)} fusion(f32[1024,512]{1,0:T(8,128)S(1)} %copy-done, f32[2048,1024]{0,1:T(8,128)S(1)} %bitcast_subtract_fusion, s32[2048]{0:T(1024)S(1)} %add_select_fusion, s32[1024]{0:T(1024)S(1)} %add_select_fusion.1), kind=kOutput, calls=%fused_computation.2 | convolution fusion | flops 6446645248 | bytes 14692352 | tf_op jit(solution)/shard_map/dot_general | solution.py:10
  178.3 3.0 pad_maximum_fusion
  181.3 0.0 all-reduce.2.cloned.1.call-start
  181.4 70.6 %reduce-scatter.2.cloned.1.call-done = f32[128,640]{0,1:T(8,128)} async-done(((f32[2048,640]{0,1:T(8,128)}), f32[128,640]{0,1:T(8,128)}) %reduce-scatter.2.cloned.1.call-update) | async-done | bytes 327696 | tf_op jit(solution)/shard_map/reduce_scatter | solution.py:40
  252.0 2.6 fusion.35
  254.6 119.2 %all-reduce.2.cloned.1.call-done = f32[512,512]{1,0:T(8,128)} async-done(((f32[512,512]{1,0:T(8,128)}), f32[512,512]{1,0:T(8,128)}) %all-reduce.2.cloned.1.call-update) | async-done | bytes 1048592 | tf_op jit(solution)/shard_map/psum | solution.py:50
  373.8 2.7 collective-permute-start
  376.6 9.2 %copy.20 = f32[2048,1024]{1,0:T(8,128)} copy(f32[2048,1024]{0,1:T(8,128)} %copy-done.1) | data formatting | bytes 16777216
  385.8 0.8 copy.21
  386.6 0.7 copy.22
  387.4 13.1 %collective-permute-done = f32[512,512]{1,0:T(8,128)} collective-permute-done((f32[512,512]{1,0:T(8,128)}, f32[512,512]{1,0:T(8,128)}, u32[]{:S(2)}, u32[]{:S(2)}) %collective-permute-start) | collective-permute-done | bytes 1048608 | tf_op jit(solution)/shard_map/ppermute | solution.py:52
  400.5 2.4 multiply_bitcast_fusion
  (40 shorter events, 0.3 us)
Async XLA Ops:
  7.2 163.5 %copy-start = (f32[1024,512]{1,0:T(8,128)S(1)}, f32[1024,512]{1,0:T(8,128)}, u32[]{:S(2)}) copy-start(f32[1024,512]{1,0:T(8,128)} %param.11) | copy-start | bytes 6291460
  7.2 77.2 %all-gather.4.cloned.1.call-start = ((), (), s32[]{:S(2)}) async-start(), calls=%async_computation.1 | async-start | bytes 4718592 | tf_op jit(solution)/shard_map/all_gather | solution.py:19
  7.9 128.2 %all-gather.6.cloned.1.call-start = ((), (), s32[]{:S(2)}) async-start(), calls=%async_computation.4 | async-start | bytes 8912896 | tf_op jit(solution)/shard_map/all_gather | solution.py:20
  8.7 243.3 %reduce-scatter.2.cloned.1.call-start = ((), (), s32[]{:S(2)}) async-start(), calls=%async_computation.2 | async-start | bytes 5570560 | tf_op jit(solution)/shard_map/reduce_scatter | solution.py:40
  8.7 9.2 %copy-start.3 = (s32[1024]{0:T(1024)S(1)}, s32[1024]{0:T(1024)}, u32[]{:S(2)}) copy-start(s32[1024]{0:T(1024)} %param.9) | copy-start | bytes 12292
  136.1 16.4 %slice-start = ((s8[8388608]{0:T(1024)(128)(4,1)}), s8[4194304]{0:T(1024)(128)(4,1)S(1)}, s32[]{:S(2)}) async-start(s8[8388608]{0:T(1024)(128)(4,1)} %bitcast.17), calls=%async_computation.5 | async-start | bytes 8388608
  144.4 8.1 %slice-start.1 = ((s8[8388608]{0:T(1024)(128)(4,1)}), s8[4194304]{0:T(1024)(128)(4,1)S(1)}, s32[]{:S(2)}) async-start(s8[8388608]{0:T(1024)(128)(4,1)} %bitcast.17), calls=%async_computation.6 | async-start | bytes 8388608
  170.4 7.9 %copy-start.1 = (f32[2048,1024]{0,1:T(8,128)}, f32[2048,1024]{0,1:T(8,128)S(1)}, u32[]{:S(2)}) copy-start(f32[2048,1024]{0,1:T(8,128)S(1)} %bitcast_subtract_fusion) | copy-start | bytes 25165828
  181.3 192.5 %all-reduce.2.cloned.1.call-start = ((), (), s32[]{:S(2)}) async-start(), calls=%async_computation.3 | async-start | bytes 2097152 | tf_op jit(solution)/shard_map/psum | solution.py:50
  254.6 131.2 %slice-start.2 = ((f32[128,640]{0,1:T(8,128)}), f32[128,512]{0,1:T(8,128)S(1)}, s32[]{:S(2)}) async-start(f32[128,640]{0,1:T(8,128)} %reduce-scatter.2.cloned.1.call-done), calls=%async_computation.7 | async-start | bytes 524288 | tf_op jit(solution)/shard_map/slice | solution.py:41
  254.6 132.0 %slice-start.3 = ((f32[128,640]{0,1:T(8,128)}), f32[128,128]{0,1:T(8,128)S(1)}, s32[]{:S(2)}) async-start(f32[128,640]{0,1:T(8,128)} %reduce-scatter.2.cloned.1.call-done), calls=%async_computation.8 | async-start | bytes 131072 | tf_op jit(solution)/shard_map/slice | solution.py:42
  373.8 26.6 %copy-start.2 = (f32[512,512]{1,0:T(8,128)S(1)}, f32[512,512]{1,0:T(8,128)}, u32[]{:S(2)}) copy-start(f32[512,512]{1,0:T(8,128)} %all-reduce.2.cloned.1.call-done) | copy-start | bytes 3145732
  373.8 26.6 %collective-permute-start = (f32[512,512]{1,0:T(8,128)}, f32[512,512]{1,0:T(8,128)}, u32[]{:S(2)}, u32[]{:S(2)}) collective-permute-start(f32[512,512]{1,0:T(8,128)} %all-reduce.2.cloned.1.call-done), channel_id=1, source_target_pairs={{0,16},{16,0},{32,48},{48,32},{64,80},{80,64},{96,112},{112,96},{1... | collective-permute-start | bytes 3145736 | tf_op jit(solution)/shard_map/ppermute | solution.py:52
Sparse Core Ops, SparseCore 0:
  10.3 74.0 all-gather.3
  86.1 49.9 all-gather.5
  181.4 70.5 reduce-scatter.1
  254.9 118.8 all-reduce.1
